TPU v7x, 32 devices: a whole 2x2x4 slice. The times are simulated.
32 devices in a mesh: wrow: 16 (over z, y, x), kblk: 2 (over core).
Axes of the slice: x: 2, y: 2, z: 4, core: 2. Of those that a mesh axis runs over, the one named last changes fastest.
Arguments:
- conduction: bfloat16 [2, 4, 64, 16384], P('kblk', None, None, 'wrow'), may hold values from -6 to 6
- valence: bfloat16 [2, 4, 64, 16384], P(None, None, 'wrow', 'kblk'), may hold values from -6 to 6
- screened: bfloat16 [4, 16384, 16384], P(None, 'wrow', 'kblk'), may hold values from -0.00036621094 to 0.00036621094
- pair_block: int32 [2, 4], replicated, may hold values from 0 to 3, as said below
Outputs:
- kernel: float32 [2, 64, 256], P('kblk', 'wrow')
Inputs may be any that keep to these rules, and one draw needn't show every extreme that they name: `pair_block`: every one of the 4 blocks is selected by at least one pair and by at most 3 pairs; one block by exactly 3 pairs.
All inputs are finite; a program needn't handle non-finite values.
Results may differ from a plain program's by a relative error of at most 0.0029.
Values may be sent and summed in bfloat16 or wider, within the bound.
No kernel may reach another device: no remote copies, remote signals or barrier semaphores. Data moves between devices by JAX's collectives and lax.ppermute only.
A program may use at most 128 MiB of HBM per device.

v0:
```python
import jax
import jax.numpy as jnp
from jax import lax
from jax.sharding import PartitionSpec as P

C = 8
V = 8


def per_device(conduction, valence, screened, pair_block):
    gathered_cond = lax.all_gather(conduction, "kblk", axis=0, tiled=True)
    gathered_vale = lax.all_gather(valence, "wrow", axis=2, tiled=True)
    k_count = gathered_cond.shape[0]
    kp_count = gathered_cond.shape[1]
    pair_count = k_count * kp_count
    row_width = gathered_cond.shape[3]
    col_width = gathered_vale.shape[3]
    cond_flat = gathered_cond.reshape(pair_count, C * C, row_width)
    vale_flat = gathered_vale.reshape(pair_count, V * V, col_width)
    flat_blocks = pair_block.reshape(pair_count)
    pair_ids = jnp.arange(pair_count, dtype=jnp.int32)
    capacity = 3 * pair_count // 8
    block_count = screened.shape[0]

    def one_block(block, total):
        sort_keys = jnp.where(flat_blocks == block, 0, pair_count) + pair_ids
        chosen = jnp.argsort(sort_keys)[:capacity]
        present = (flat_blocks[chosen] == block).astype(jnp.float32)
        vale_sel = jnp.take(vale_flat, chosen, axis=0)
        cond_sel = jnp.take(cond_flat, chosen, axis=0)
        w_tile = lax.dynamic_index_in_dim(screened, block, 0, keepdims=False)
        screened_vale = jnp.einsum(
            "pvh,gh->pvg", vale_sel, w_tile, preferred_element_type=jnp.float32
        ).astype(jnp.bfloat16)
        tiles = jnp.einsum(
            "pcg,pvg->pcv", cond_sel, screened_vale, preferred_element_type=jnp.float32
        )
        placer = (pair_ids[:, None] == chosen[None, :]).astype(jnp.float32) * present[None, :]
        return total + jnp.einsum("sp,pcv->scv", placer, tiles, precision=lax.Precision.HIGHEST)

    terms = lax.fori_loop(
        0, block_count, one_block, jnp.zeros((pair_count, C * C, V * V), jnp.float32)
    )
    terms = terms.reshape(k_count, kp_count, C, C, V, V).transpose(0, 2, 4, 1, 3, 5)
    terms = terms.reshape(k_count, C * V, kp_count * C * V)
    by_block = lax.psum_scatter(terms, "kblk", scatter_dimension=0, tiled=True)
    return lax.psum_scatter(by_block, "wrow", scatter_dimension=1, tiled=True)


def solution(mesh):
    return jax.shard_map(
        per_device,
        mesh=mesh,
        in_specs=(
            P("kblk", None, None, "wrow"),
            P(None, None, "wrow", "kblk"),
            P(None, "wrow", "kblk"),
            P(),
        ),
        out_specs=P("kblk", "wrow", None),
        check_vma=False,
    )
```

profile of v0, /device:TPU:0, one launch (start us, length us, event | category | flops | bytes accessed | tf_op | source)
XLA Modules:
  0.0 346.6 jit_solution(13563379429917125649)
XLA Ops:
  6.5 2.2 copy.8
  10.4 114.8 %all-gather.5.cloned.1.call-done = bf16[2,4,64,8192]{3,1,0,2:T(4,128)(2,1)} async-done(((bf16[2,4,4,8192]{3,1,0,2:T(4,128)(2,1)}), bf16[2,4,64,8192]{3,1,0,2:T(4,128)(2,1)}) %all-gather.5.cloned.1.call-update) | async-done | bytes 8388624 | tf_op jit(solution)/shard_map/all_gather | solution.py:12
  125.2 11.2 %copy.11 = bf16[2,4,64,8192]{3,2,1,0:T(8,128)(2,1)} copy(bf16[2,4,64,8192]{3,1,0,2:T(4,128)(2,1)} %all-gather.5.cloned.1.call-done) | data formatting | bytes 16777216
  136.3 78.8 %while.15 = (s32[]{:T(128)}, f32[8,64,64]{2,0,1:T(8,128)S(1)}, s32[8]{0:T(128)S(1)}, bf16[8,64,1024]{2,1,0:T(8,128)(2,1)}, bf16[8,64,8192]{2,1,0:T(8,128)(2,1)},...) while((s32[]{:T(128)}, f32[8,64,64]{2,0,1:T(8,128)S(1)}, s32[8]{0:T(128)S(1)}, ...), condition=%wide.region_2.3_spmd.clone.clone, body=%wide.region_0.2_spmd.clone.clone.sunk | while | flops 3249603584 | bytes 28546016 | solution.py:41
  137.3 4.1 %gather_fusion = bf16[3,64,8192]{2,1,0:T(8,128)(2,1)S(1)} fusion(bf16[8,64,8192]{2,1,0:T(8,128)(2,1)} %get-tuple-element.260, s32[1024]{0:T(1024)S(1)} %pad_clamp_fusion.2), kind=kCustom, calls=%fused_computation.2.clone.clone.1 | custom fusion | bytes 6291468 | tf_op jit(solution)/shard_map/while/body/eval_jaxpr/jit(_take)/gather | solution.py:29
  141.5 10.3 %fusion.45 = bf16[3,64,1024]{2,1,0:T(8,128)(2,1)} fusion(bf16[4,1024,8192]{2,1,0:T(8,128)(2,1)} %get-tuple-element.261, s32[]{:T(128)} %get-tuple-element.248, bf16[3,64,8192]{2,1,0:T(8,128)(2,1)S(1)} %gather_fusion, pred[3]{0:T(512)(128)(4,1)S(1)} %get-tuple-element.239), kind=kOutput, calls=%fused_computation.10.clone.1 | convolution fusion | flops 3222994944 | bytes 20316676 | tf_op jit(solution)/shard_map/while/body/eval_jaxpr/pvh,gh->pvg/dot_general | solution.py:32
  151.8 1.8 gather_fusion.1
  153.6 1.3 fusion.46
  157.1 4.1 %gather_fusion = bf16[3,64,8192]{2,1,0:T(8,128)(2,1)S(1)} fusion(bf16[8,64,8192]{2,1,0:T(8,128)(2,1)} %get-tuple-element.260, s32[1024]{0:T(1024)S(1)} %pad_clamp_fusion.2), kind=kCustom, calls=%fused_computation.2.clone.clone.1 | custom fusion | bytes 6291468 | tf_op jit(solution)/shard_map/while/body/eval_jaxpr/jit(_take)/gather | solution.py:29
  161.2 10.3 %fusion.45 = bf16[3,64,1024]{2,1,0:T(8,128)(2,1)} fusion(bf16[4,1024,8192]{2,1,0:T(8,128)(2,1)} %get-tuple-element.261, s32[]{:T(128)} %get-tuple-element.248, bf16[3,64,8192]{2,1,0:T(8,128)(2,1)S(1)} %gather_fusion, pred[3]{0:T(512)(128)(4,1)S(1)} %get-tuple-element.239), kind=kOutput, calls=%fused_computation.10.clone.1 | convolution fusion | flops 3222994944 | bytes 20316676 | tf_op jit(solution)/shard_map/while/body/eval_jaxpr/pvh,gh->pvg/dot_general | solution.py:32
  171.5 1.8 gather_fusion.1
  173.3 1.3 fusion.46
  176.8 4.1 %gather_fusion = bf16[3,64,8192]{2,1,0:T(8,128)(2,1)S(1)} fusion(bf16[8,64,8192]{2,1,0:T(8,128)(2,1)} %get-tuple-element.260, s32[1024]{0:T(1024)S(1)} %pad_clamp_fusion.2), kind=kCustom, calls=%fused_computation.2.clone.clone.1 | custom fusion | bytes 6291468 | tf_op jit(solution)/shard_map/while/body/eval_jaxpr/jit(_take)/gather | solution.py:29
  180.9 10.3 %fusion.45 = bf16[3,64,1024]{2,1,0:T(8,128)(2,1)} fusion(bf16[4,1024,8192]{2,1,0:T(8,128)(2,1)} %get-tuple-element.261, s32[]{:T(128)} %get-tuple-element.248, bf16[3,64,8192]{2,1,0:T(8,128)(2,1)S(1)} %gather_fusion, pred[3]{0:T(512)(128)(4,1)S(1)} %get-tuple-element.239), kind=kOutput, calls=%fused_computation.10.clone.1 | convolution fusion | flops 3222994944 | bytes 20316676 | tf_op jit(solution)/shard_map/while/body/eval_jaxpr/pvh,gh->pvg/dot_general | solution.py:32
  191.2 1.8 gather_fusion.1
  193.0 1.3 fusion.46
  196.5 4.1 %gather_fusion = bf16[3,64,8192]{2,1,0:T(8,128)(2,1)S(1)} fusion(bf16[8,64,8192]{2,1,0:T(8,128)(2,1)} %get-tuple-element.260, s32[1024]{0:T(1024)S(1)} %pad_clamp_fusion.2), kind=kCustom, calls=%fused_computation.2.clone.clone.1 | custom fusion | bytes 6291468 | tf_op jit(solution)/shard_map/while/body/eval_jaxpr/jit(_take)/gather | solution.py:29
  200.6 10.3 %fusion.45 = bf16[3,64,1024]{2,1,0:T(8,128)(2,1)} fusion(bf16[4,1024,8192]{2,1,0:T(8,128)(2,1)} %get-tuple-element.261, s32[]{:T(128)} %get-tuple-element.248, bf16[3,64,8192]{2,1,0:T(8,128)(2,1)S(1)} %gather_fusion, pred[3]{0:T(512)(128)(4,1)S(1)} %get-tuple-element.239), kind=kOutput, calls=%fused_computation.10.clone.1 | convolution fusion | flops 3222994944 | bytes 20316676 | tf_op jit(solution)/shard_map/while/body/eval_jaxpr/pvh,gh->pvg/dot_general | solution.py:32
  210.9 1.8 gather_fusion.1
  212.7 1.3 fusion.46
  215.8 3.0 copy.17
  218.8 3.5 reshape.32
  222.3 6.4 %reduce-scatter.3.cloned.1.call-done = f32[1,64,256]{2,1,0:T(8,128)} async-done(((f32[2,64,256]{2,1,0:T(8,128)}), f32[1,64,256]{2,1,0:T(8,128)}) %reduce-scatter.3.cloned.1.call-update) | async-done | bytes 65552 | tf_op jit(solution)/shard_map/reduce_scatter | solution.py:46
  230.0 108.7 %all-reduce.3.cloned.1.call-done = f32[1,64,256]{2,1,0:T(8,128)} async-done(((f32[1,64,256]{2,1,0:T(8,128)}), f32[1,64,256]{2,1,0:T(8,128)}) %all-reduce.3.cloned.1.call-update) | async-done | bytes 65552
  (48 shorter events, 12.7 us)
Async XLA Ops:
  6.5 118.6 %all-gather.5.cloned.1.call-start = ((), (), s32[]{:S(2)}) async-start(), calls=%async_computation.2 | async-start | bytes 8912896 | tf_op jit(solution)/shard_map/all_gather | solution.py:12
  8.8 127.6 %all-gather.3.cloned.1.call-start = ((), (), s32[]{:S(2)}) async-start(), calls=%async_computation.1 | async-start | bytes 1572864 | tf_op jit(solution)/shard_map/all_gather | solution.py:11
  9.5 219.2 %reduce-scatter.3.cloned.1.call-start = ((), (), s32[]{:S(2)}) async-start(), calls=%async_computation.3 | async-start | bytes 196608 | tf_op jit(solution)/shard_map/reduce_scatter | solution.py:46
  215.8 13.0 %copy-start = (u32[32]{0:T(128)S(1)}, u32[32]{0:T(128)}, u32[]{:S(2)}) copy-start(u32[32]{0:T(128)} %constant.81) | copy-start | bytes 388
  222.2 116.5 %all-reduce.3.cloned.1.call-start = ((), (), s32[]{:S(2)}) async-start(), calls=%async_computation.4 | async-start | bytes 131072
Sparse Core Ops, SparseCore 0:
  10.1 115.0 all-gather.4
  126.7 7.1 all-gather.2
  222.4 6.3 reduce-scatter.2
  234.1 104.6 all-reduce.2
where the time goes:
time: 347 us
  waiting for transfers between devices  231 us (67%)
  local copies, waits for them, and re-layouts  49.3 us (14%)
  matrix products  48.4 us (14%)
  between operations  13.8 us (4%)
  other arithmetic  3.96 us (1%)
    all_gather x1, waiting for transfers between devices, per_device(): gathered_vale = lax.all_gather(valence, 'wrow', axis=2, tiled=True)  115 us
    unnamed x5, waiting for transfers between devices  109 us
    dot_general x4, matrix products, one_block(): jnp.einsum('pvh,gh->pvg', vale_sel, w_tile, preferred_element_type=jnp.fl...  41.1 us
    gather x4, local copies, waits for them, and re-layouts, one_block(): vale_sel = jnp.take(vale_flat, chosen, axis=0)  16.5 us
    unnamed x6, local copies, waits for them, and re-layouts  15.3 us
    gather x4, local copies, waits for them, and re-layouts, one_block(): cond_sel = jnp.take(cond_flat, chosen, axis=0)  7.18 us
  transfers between devices with their start and end apart: 4, of which 3 were waited for; matrix products, arithmetic and copies ran while one was open for 4% of the time, Pallas kernels for 0%

commit v1 on v0

--- a/solution.py
+++ b/solution.py
@@ -7,9 +7,21 @@
 V = 8
 
 
+def doubled_up(array, axis, dim):
+    ways, here, lap = (lax.axis_size(axis), lax.axis_index(axis), array.shape[dim])
+    line, have = (array, 1)
+    while have < ways:
+        line = jnp.concatenate(
+            [line, lax.ppermute(line, axis, [(d, (d - have) % ways) for d in range(ways)])],
+            axis=dim,
+        )
+        have = 2 * have
+    return jnp.roll(line, here * lap, axis=dim)
+
+
 def per_device(conduction, valence, screened, pair_block):
     gathered_cond = lax.all_gather(conduction, "kblk", axis=0, tiled=True)
-    gathered_vale = lax.all_gather(valence, "wrow", axis=2, tiled=True)
+    gathered_vale = doubled_up(valence, "wrow", 2)
     k_count = gathered_cond.shape[0]
     kp_count = gathered_cond.shape[1]
     pair_count = k_count * kp_count

time: 347 us -> 572 us (1.65)
  waiting for transfers between devices: 231 us -> 381 us
  local copies, waits for them, and re-layouts: 49.3 us -> 107 us
  starting transfers between devices: 0.12 us -> 9.1 us
  other arithmetic: 3.96 us -> 10.1 us
    ppermute x0 -> x4, waiting for transfers between devices: none -> 260 us  [doubled_up(): lax.ppermute(line, axis, [(d, (d - have) % ways) for d in range(ways)])]
    all_gather x1 -> x0, waiting for transfers between devices: 115 us -> none  [per_device(): gathered_vale = lax.all_gather(valence, 'wrow', axis=2, tiled=True)]
    concatenate x0 -> x1, local copies, waits for them, and re-layouts: none -> 62.4 us  [doubled_up(): return jnp.roll(line, here * lap, axis=dim)]
    unnamed x6 -> x10, local copies, waits for them, and re-layouts: 15.3 us -> 1.9 us
    ppermute x0 -> x4, starting transfers between devices: none -> 9.01 us  [doubled_up(): lax.ppermute(line, axis, [(d, (d - have) % ways) for d in range(ways)])]
    dynamic_slice x0 -> x1, local copies, waits for them, and re-layouts: none -> 8.96 us  [doubled_up(): return jnp.roll(line, here * lap, axis=dim)]
    reduce_scatter x1, waiting for transfers between devices: 6.44 us -> 12.8 us  [per_device(): by_block = lax.psum_scatter(terms, 'kblk', scatter_dimension=0, tiled=True)]
    concatenate x0 -> x3, other arithmetic: none -> 6.22 us  [doubled_up(): jnp.concatenate([line, lax.ppermute(line, axis, [(d, (d - have) % ways) f...]
  transfers between devices with their start and end apart: 4 -> 7, of which waited for: 3 -> 6; matrix products, arithmetic and copies ran while one was open for 4% -> 13% of each run, Pallas kernels for 0% -> 0%
where the time goes in v1:
time: 572 us; the launch traced here: 569 us
  waiting for transfers between devices  381 us (67%)
  local copies, waits for them, and re-layouts  107 us (19%)
  matrix products  48.2 us (8%)
  between operations  13.9 us (2%)
  other arithmetic  10.1 us (2%)
  starting transfers between devices  9.1 us (2%)
    ppermute x4, waiting for transfers between devices, doubled_up(): lax.ppermute(line, axis, [(d, (d - have) % ways) for d in range(ways)])  260 us
    unnamed x4, waiting for transfers between devices  109 us
    concatenate x1, local copies, waits for them, and re-layouts, doubled_up(): return jnp.roll(line, here * lap, axis=dim)  62.4 us
    dot_general x4, matrix products, one_block(): jnp.einsum('pvh,gh->pvg', vale_sel, w_tile, preferred_element_type=jnp.fl...  40.9 us
    gather x4, local copies, waits for them, and re-layouts, one_block(): vale_sel = jnp.take(vale_flat, chosen, axis=0)  16.5 us
    reduce_scatter x1, waiting for transfers between devices, per_device(): by_block = lax.psum_scatter(terms, 'kblk', scatter_dimension=0, tiled=True)  12.8 us
  transfers between devices with their start and end apart: 7, of which 6 were waited for; matrix products, arithmetic and copies ran while one was open for 13% of the time, Pallas kernels for 0%

profile of v1, /device:TPU:0, one launch (start us, length us, event | category | flops | bytes accessed | tf_op | source)
XLA Modules:
  0.0 569.3 jit_solution(16578556280611589363)
XLA Ops:
  6.5 7.0 %collective-permute-start = (bf16[2,4,4,8192]{3,2,1,0:T(4,128)(2,1)}, bf16[2,4,4,8192]{3,2,1,0:T(4,128)(2,1)S(1)}, u32[]{:S(2)}, u32[]{:S(2)}) collective-permute-start(bf16[2,4,4,8192]{3,2,1,0:T(4,128)(2,1)} %param.7), channel_id=1, source_target_pairs={{0,30},{2,0},{4,2},{6,4},{8,6},{10,8},{12,10},{14,12},{16,14},{18,... | collective-permute-start | bytes 1572872 | tf_op jit(solution)/shard_map/ppermute | solution.py:15
  13.5 11.5 %collective-permute-done = bf16[2,4,4,8192]{3,2,1,0:T(4,128)(2,1)S(1)} collective-permute-done((bf16[2,4,4,8192]{3,2,1,0:T(4,128)(2,1)}, bf16[2,4,4,8192]{3,2,1,0:T(4,128)(2,1)S(1)}, u32[]{:S(2)}, u32[]{:S(2)}) %collective-permute-start) | collective-permute-done | bytes 524320 | tf_op jit(solution)/shard_map/ppermute | solution.py:15
  28.2 22.6 %collective-permute-done.1 = bf16[2,4,8,8192]{3,2,1,0:T(8,128)(2,1)S(1)} collective-permute-done((bf16[2,4,8,8192]{3,2,1,0:T(8,128)(2,1)S(1)}, bf16[2,4,8,8192]{3,2,1,0:T(8,128)(2,1)S(1)}, u32[]{:S(2)}, u32[]{:S(2)}) %collective-permute-start.1) | collective-permute-done | bytes 1048608 | tf_op jit(solution)/shard_map/ppermute | solution.py:15
  50.8 1.9 pad_maximum_fusion.1
  53.3 45.2 %collective-permute-done.2 = bf16[2,4,16,8192]{3,2,1,0:T(8,128)(2,1)S(1)} collective-permute-done((bf16[2,4,16,8192]{3,2,1,0:T(8,128)(2,1)S(1)}, bf16[2,4,16,8192]{3,2,1,0:T(8,128)(2,1)S(1)}, u32[]{:S(2)}, u32[]{:S(2)}) %collective-permute-start.2) | collective-permute-done | bytes 2097184 | tf_op jit(solution)/shard_map/ppermute | solution.py:15
  98.5 2.6 pad_maximum_fusion
  101.3 180.3 %collective-permute-done.3 = bf16[2,4,32,8192]{3,2,1,0:T(8,128)(2,1)} collective-permute-done((bf16[2,4,32,8192]{3,2,1,0:T(8,128)(2,1)}, bf16[2,4,32,8192]{3,2,1,0:T(8,128)(2,1)}, u32[]{:S(2)}, u32[]{:S(2)}) %collective-permute-start.3) | collective-permute-done | bytes 4194336 | tf_op jit(solution)/shard_map/ppermute | solution.py:15
  281.6 62.4 %concatenate.21 = bf16[2,4,128,8192]{3,2,1,0:T(8,128)(2,1)} concatenate(bf16[2,4,4,8192]{3,2,1,0:T(4,128)(2,1)} %param.7, bf16[2,4,4,8192]{3,2,1,0:T(4,128)(2,1)} %copy-done.1, bf16[2,4,8,8192]{3,2,1,0:T(8,128)(2,1)S(1)} %collective-permute-done.1, bf16[2,4,16,8192]{3,2,1,0:T(8,128)(2,1)S(1)} %collective-permute-done.2, bf16[2,4,32,8192]{3,2,1,0:T(8,128)(2,1)} %collective-permute-done.3, ...), dimensions={2} | concatenate | bytes 33554432 | tf_op jit(solution)/shard_map/jit(_roll_dynamic)/concatenate | solution.py:19
  343.9 9.0 %constant_dynamic-slice_fusion.1 = bf16[2,4,64,8192]{3,2,1,0:T(8,128)(2,1)} fusion(bf16[2,4,128,8192]{3,2,1,0:T(8,128)(2,1)} %concatenate.21, s32[]{:T(128)S(6)} %select_n.56), kind=kLoop, calls=%fused_computation.38 | loop fusion | bytes 16777220 | tf_op jit(solution)/shard_map/jit(_roll_dynamic)/dynamic_slice | solution.py:19
  352.9 78.6 %while.15 = (s32[]{:T(128)}, f32[8,64,64]{2,0,1:T(8,128)S(1)}, s32[8]{0:T(128)S(1)}, bf16[8,64,1024]{2,1,0:T(8,128)(2,1)}, bf16[8,64,8192]{2,1,0:T(8,128)(2,1)},...) while((s32[]{:T(128)}, f32[8,64,64]{2,0,1:T(8,128)S(1)}, s32[8]{0:T(128)S(1)}, ...), condition=%wide.region_2.3_spmd.clone.clone, body=%wide.region_0.2_spmd.clone.clone.sunk | while | flops 3249603584 | bytes 28546016 | solution.py:53
  353.9 4.1 gather_fusion
  358.0 10.2 %fusion.45 = bf16[3,64,1024]{2,1,0:T(8,128)(2,1)} fusion(bf16[4,1024,8192]{2,1,0:T(8,128)(2,1)} %get-tuple-element.255, s32[]{:T(128)} %get-tuple-element.242, bf16[3,64,8192]{2,1,0:T(8,128)(2,1)S(1)} %gather_fusion, pred[3]{0:T(512)(128)(4,1)S(1)} %get-tuple-element.233), kind=kOutput, calls=%fused_computation.10.clone.1 | convolution fusion | flops 3222994944 | bytes 20316676 | tf_op jit(solution)/shard_map/while/body/eval_jaxpr/pvh,gh->pvg/dot_general | solution.py:44
  368.2 1.8 gather_fusion.1
  373.5 4.1 gather_fusion
  377.7 10.2 %fusion.45 = bf16[3,64,1024]{2,1,0:T(8,128)(2,1)} fusion(bf16[4,1024,8192]{2,1,0:T(8,128)(2,1)} %get-tuple-element.255, s32[]{:T(128)} %get-tuple-element.242, bf16[3,64,8192]{2,1,0:T(8,128)(2,1)S(1)} %gather_fusion, pred[3]{0:T(512)(128)(4,1)S(1)} %get-tuple-element.233), kind=kOutput, calls=%fused_computation.10.clone.1 | convolution fusion | flops 3222994944 | bytes 20316676 | tf_op jit(solution)/shard_map/while/body/eval_jaxpr/pvh,gh->pvg/dot_general | solution.py:44
  387.9 1.8 gather_fusion.1
  393.2 4.1 gather_fusion
  397.3 10.2 %fusion.45 = bf16[3,64,1024]{2,1,0:T(8,128)(2,1)} fusion(bf16[4,1024,8192]{2,1,0:T(8,128)(2,1)} %get-tuple-element.255, s32[]{:T(128)} %get-tuple-element.242, bf16[3,64,8192]{2,1,0:T(8,128)(2,1)S(1)} %gather_fusion, pred[3]{0:T(512)(128)(4,1)S(1)} %get-tuple-element.233), kind=kOutput, calls=%fused_computation.10.clone.1 | convolution fusion | flops 3222994944 | bytes 20316676 | tf_op jit(solution)/shard_map/while/body/eval_jaxpr/pvh,gh->pvg/dot_general | solution.py:44
  412.8 4.1 gather_fusion
  417.0 10.2 %fusion.45 = bf16[3,64,1024]{2,1,0:T(8,128)(2,1)} fusion(bf16[4,1024,8192]{2,1,0:T(8,128)(2,1)} %get-tuple-element.255, s32[]{:T(128)} %get-tuple-element.242, bf16[3,64,8192]{2,1,0:T(8,128)(2,1)S(1)} %gather_fusion, pred[3]{0:T(512)(128)(4,1)S(1)} %get-tuple-element.233), kind=kOutput, calls=%fused_computation.10.clone.1 | convolution fusion | flops 3222994944 | bytes 20316676 | tf_op jit(solution)/shard_map/while/body/eval_jaxpr/pvh,gh->pvg/dot_general | solution.py:44
  432.1 3.0 copy.14
  435.1 3.4 reshape.32
  438.6 12.8 %reduce-scatter.3.cloned.1.call-done = f32[1,64,256]{2,1,0:T(8,128)} async-done(((f32[2,64,256]{2,1,0:T(8,128)}), f32[1,64,256]{2,1,0:T(8,128)}) %reduce-scatter.3.cloned.1.call-update) | async-done | bytes 65552 | tf_op jit(solution)/shard_map/reduce_scatter | solution.py:58
  452.6 108.8 %all-reduce.3.cloned.1.call-done = f32[1,64,256]{2,1,0:T(8,128)} async-done(((f32[1,64,256]{2,1,0:T(8,128)}), f32[1,64,256]{2,1,0:T(8,128)}) %all-reduce.3.cloned.1.call-update) | async-done | bytes 65552
  (62 shorter events, 23.9 us)
Async XLA Ops:
  6.5 346.4 %all-gather.2.cloned.1.call-start = ((), (), s32[]{:S(2)}) async-start(), calls=%async_computation.1 | async-start | bytes 1572864 | tf_op jit(solution)/shard_map/all_gather | solution.py:23
  6.5 91.9 %copy-start = (bf16[2,4,4,8192]{3,2,1,0:T(4,128)(2,1)S(1)}, bf16[2,4,4,8192]{3,2,1,0:T(4,128)(2,1)}, u32[]{:S(2)}) copy-start(bf16[2,4,4,8192]{3,2,1,0:T(4,128)(2,1)} %param.7) | copy-start | bytes 1572868
  6.5 18.5 %collective-permute-start = (bf16[2,4,4,8192]{3,2,1,0:T(4,128)(2,1)}, bf16[2,4,4,8192]{3,2,1,0:T(4,128)(2,1)S(1)}, u32[]{:S(2)}, u32[]{:S(2)}) collective-permute-start(bf16[2,4,4,8192]{3,2,1,0:T(4,128)(2,1)} %param.7), channel_id=1, source_target_pairs={{0,30},{2,0},{4,2},{6,4},{8,6},{10,8},{12,10},{14,12},{16,14},{18,... | collective-permute-start | bytes 1572872 | tf_op jit(solution)/shard_map/ppermute | solution.py:15
  25.0 76.1 %copy-start.1 = (bf16[2,4,4,8192]{3,2,1,0:T(4,128)(2,1)}, bf16[2,4,4,8192]{3,2,1,0:T(4,128)(2,1)S(1)}, u32[]{:S(2)}) copy-start(bf16[2,4,4,8192]{3,2,1,0:T(4,128)(2,1)S(1)} %collective-permute-done) | copy-start | bytes 1572868
  26.7 24.1 %collective-permute-start.1 = (bf16[2,4,8,8192]{3,2,1,0:T(8,128)(2,1)S(1)}, bf16[2,4,8,8192]{3,2,1,0:T(8,128)(2,1)S(1)}, u32[]{:S(2)}, u32[]{:S(2)}) collective-permute-start(bf16[2,4,8,8192]{3,2,1,0:T(8,128)(2,1)S(1)} %pad_maximum_fusion.2), channel_id=1, source_target_pairs={{0,28},{2,30},{4,0},{6,2},{8,4},{10,6},{12,8},{14,10},{16,12},{18,... | collective-permute-start | bytes 3145736 | tf_op jit(solution)/shard_map/ppermute | solution.py:15
  52.7 48.5 %copy-start.2 = (s32[2,4]{1,0:T(2,128)S(1)}, s32[2,4]{1,0:T(2,128)}, u32[]{:S(2)}) copy-start(s32[2,4]{1,0:T(2,128)} %param.9) | copy-start | bytes 100
  52.7 45.7 %collective-permute-start.2 = (bf16[2,4,16,8192]{3,2,1,0:T(8,128)(2,1)S(1)}, bf16[2,4,16,8192]{3,2,1,0:T(8,128)(2,1)S(1)}, u32[]{:S(2)}, u32[]{:S(2)}) collective-permute-start(bf16[2,4,16,8192]{3,2,1,0:T(8,128)(2,1)S(1)} %pad_maximum_fusion.1), channel_id=1, source_target_pairs={{0,24},{2,26},{4,28},{6,30},{8,0},{10,2},{12,4},{14,6},{16,8},{18,... | collective-permute-start | bytes 6291464 | tf_op jit(solution)/shard_map/ppermute | solution.py:15
  101.1 180.5 %collective-permute-start.3 = (bf16[2,4,32,8192]{3,2,1,0:T(8,128)(2,1)}, bf16[2,4,32,8192]{3,2,1,0:T(8,128)(2,1)}, u32[]{:S(2)}, u32[]{:S(2)}) collective-permute-start(bf16[2,4,32,8192]{3,2,1,0:T(8,128)(2,1)} %pad_maximum_fusion), channel_id=1, source_target_pairs={{0,16},{2,18},{4,20},{6,22},{8,24},{10,26},{12,28},{14,30},{16,0},... | collective-permute-start | bytes 12582920 | tf_op jit(solution)/shard_map/ppermute | solution.py:15
  101.1 350.3 %reduce-scatter.3.cloned.1.call-start = ((), (), s32[]{:S(2)}) async-start(), calls=%async_computation.2 | async-start | bytes 196608 | tf_op jit(solution)/shard_map/reduce_scatter | solution.py:58
  431.5 19.9 %copy-start.3 = (u32[32]{0:T(128)S(1)}, u32[32]{0:T(128)}, u32[]{:S(2)}) copy-start(u32[32]{0:T(128)} %constant.110) | copy-start | bytes 388
  438.6 122.9 %all-reduce.3.cloned.1.call-start = ((), (), s32[]{:S(2)}) async-start(), calls=%async_computation.3 | async-start | bytes 131072
Sparse Core Ops, SparseCore 0:
  101.2 15.8 all-gather.1
  438.7 12.6 reduce-scatter.2
  456.9 104.5 all-reduce.2
